TPU v7x, 128 devices: a whole 4x4x4 slice. The times are simulated.
128 devices in a mesh: dp: 8 (over y, x_hi), section: 4 (over x_lo, core), mp: 4 (over z).
Axes of the slice: x: 4 (x_hi: 2, x_lo: 2; x = x_hi * 2 + x_lo), y: 4, z: 4, core: 2. Of those that a mesh axis runs over, the one named last changes fastest.
Arguments:
- hidden_in: bfloat16 [16, 128, 4096], P('dp')
- slot_hidden: bfloat16 [4, 16, 16, 4096], P('section', 'dp'), may hold values from -6 to 6
- norm_gain: float32 [4, 4096], P('section'), may hold values from 0.5 to 1.5
- w_query: bfloat16 [4, 4096, 3072], P('section', None, 'mp')
- w_key: bfloat16 [4, 4096, 1024], P('section', None, 'mp')
- w_value: bfloat16 [4, 4096, 1024], P('section', None, 'mp'), may hold values from -0.09375 to 0.09375
- w_out: bfloat16 [4, 3072, 4096], P('section', 'mp'), may hold values from -0.109375 to 0.109375
- key_a: bfloat16 [4, 4096, 64], P('section'), may hold values from -0.09375 to 0.09375
- key_b: bfloat16 [4, 64, 1024], P('section', None, 'mp'), may hold values from -0.375 to 0.375
- value_a: bfloat16 [4, 4096, 64], P('section'), may hold values from -0.09375 to 0.09375
- value_b: bfloat16 [4, 64, 1024], P('section', None, 'mp'), may hold values from -0.375 to 0.375
- cotangent: bfloat16 [16, 128, 4096], P('dp'), may hold values from -6 to 6
Outputs:
- grad_a: float32 [4, 2, 4096, 64], P('section')
- grad_b: float32 [4, 2, 64, 1024], P('section', None, None, 'mp')
All inputs are finite; a program needn't handle non-finite values.
Results may differ from a plain program's by a relative error of at most 0.028.
Values may be sent and summed in bfloat16 or wider, within the bound.
No kernel may reach another device: no remote copies, remote signals or barrier semaphores. Data moves between devices by JAX's collectives and lax.ppermute only.
A program may use at most 128 MiB of HBM per device.

v0:
```python
import math
import jax
import jax.numpy as jnp
from jax import lax
from jax.sharding import PartitionSpec as P

HD = 128
SLOTS = 16
MICRO = 2
EPS = 1e-05
NEG = -1e30
HIGH = lax.Precision.HIGHEST


def in_blocks(array, dim, length):
    before, after = (array.shape[:dim], array.shape[dim + 1 :])
    return jnp.moveaxis(array.reshape(*before, length, -1, *after), dim, 0)


def summed_on_arrival(array, axis, dim):
    length = lax.axis_size(axis)
    pieces = lax.all_to_all(in_blocks(array, dim, length), axis, 0, 0, tiled=True)
    return jnp.sum(pieces, axis=0)


def laid_out(pieces, dim):
    shape = list(pieces.shape[1:])
    shape[dim] *= pieces.shape[0]
    return jnp.moveaxis(pieces, 0, dim).reshape(shape)


def copy_for_each(array, axis):
    copies = jnp.broadcast_to(array, (lax.axis_size(axis), *array.shape))
    return lax.all_to_all(copies, axis, split_axis=0, concat_axis=0, tiled=True)


def collect(array, axis, dim):
    return laid_out(copy_for_each(array, axis), dim)


def passed_along(block, axis, distance):
    devices = range(lax.axis_size(axis))
    route = [(i - distance, i) for i in devices if i - distance in devices]
    return lax.ppermute(block, axis, route)


def sent_and_summed(array, axis, dim):
    pieces = in_blocks(array, dim, lax.axis_size(axis))
    arrived = lax.all_to_all(pieces, axis, split_axis=0, concat_axis=0, tiled=True)
    return arrived.astype(jnp.float32).sum(axis=0)


def taken_together(array, axis):
    everything = copy_for_each(array, axis)
    return jnp.sum(everything, axis=0)


def normalize(rows):
    wide = rows.astype(jnp.float32)
    inverse = lax.rsqrt(jnp.mean(wide * wide, axis=-1, keepdims=True) + EPS)
    return (wide * inverse, inverse)


def visible(count, slots):
    qpos = lax.broadcasted_iota(jnp.int32, (count, slots + count), 0)
    kpos = lax.broadcasted_iota(jnp.int32, (count, slots + count), 1)
    return (kpos < slots) | (kpos - slots <= qpos)


def mixdot(left, right):
    return jnp.dot(left, right, preferred_element_type=jnp.float32)


def attend(query, keys, values):
    count = query.shape[0]
    groups = keys.shape[1] // HD
    per_group = query.shape[1] // keys.shape[1]
    q_four = query.reshape(count, groups, per_group, HD)
    k_three = keys.reshape(-1, groups, HD)
    v_three = values.reshape(-1, groups, HD)
    scores = jnp.einsum(
        "igcd,jgd->gcij", q_four, k_three, preferred_element_type=jnp.float32
    ) / math.sqrt(HD)
    scores = jnp.where(visible(count, SLOTS), scores, NEG)
    top = jnp.max(scores, axis=-1, keepdims=True)
    probs = jnp.exp(scores - top)
    probs = probs / jnp.sum(probs, axis=-1, keepdims=True)
    weights = probs.astype(jnp.bfloat16)
    mixed = jnp.einsum("gcij,jgd->igcd", weights, v_three, preferred_element_type=jnp.float32)
    return (mixed.reshape(count, -1).astype(jnp.bfloat16), probs, weights)


def attend_back(grad_mixed, query, keys, values, probs, weights):
    count = query.shape[0]
    groups = keys.shape[1] // HD
    per_group = query.shape[1] // keys.shape[1]
    q_four = query.reshape(count, groups, per_group, HD)
    k_three = keys.reshape(-1, groups, HD)
    v_three = values.reshape(-1, groups, HD)
    g_four = grad_mixed.reshape(count, groups, per_group, HD)
    grad_probs = jnp.einsum("igcd,jgd->gcij", g_four, v_three, preferred_element_type=jnp.float32)
    grad_values = jnp.einsum("gcij,igcd->jgd", weights, g_four, preferred_element_type=jnp.float32)
    grad_scores = probs * (grad_probs - jnp.sum(probs * grad_probs, axis=-1, keepdims=True))
    scaled = (grad_scores / math.sqrt(HD)).astype(jnp.bfloat16)
    grad_query = jnp.einsum("gcij,jgd->igcd", scaled, k_three, preferred_element_type=jnp.float32)
    grad_keys = jnp.einsum("gcij,igcd->jgd", scaled, q_four, preferred_element_type=jnp.float32)
    return (
        grad_query.reshape(count, -1).astype(jnp.bfloat16),
        grad_keys.reshape(-1, groups * HD),
        grad_values.reshape(-1, groups * HD),
    )


def slot_entries(slot_rows, gain, w_key, w_value, key_a, key_b, value_a, value_b):
    unit, inverse = normalize(slot_rows)
    slot_normed = (unit * gain).astype(jnp.bfloat16)
    low_key = mixdot(slot_normed, key_a).astype(jnp.bfloat16)
    low_value = mixdot(slot_normed, value_a).astype(jnp.bfloat16)
    slot_keys = (mixdot(slot_normed, w_key) + mixdot(low_key, key_b)).astype(jnp.bfloat16)
    slot_values = (mixdot(slot_normed, w_value) + mixdot(low_value, value_b)).astype(jnp.bfloat16)
    return (slot_normed, low_key, low_value, slot_keys, slot_values)


def local(
    hidden_in,
    slot_hidden,
    norm_gain,
    w_query,
    w_key,
    w_value,
    w_out,
    key_a,
    key_b,
    value_a,
    value_b,
    cotangent,
):
    gain = norm_gain[0]
    w_q = w_query[0]
    w_k = w_key[0]
    w_v = w_value[0]
    w_o = w_out[0]
    down_key = key_a[0]
    up_key = key_b[0]
    down_value = value_a[0]
    up_value = value_b[0]
    slot_all = slot_hidden[0]
    section = lax.axis_index("section")
    sections = lax.axis_size("section")
    ticks = MICRO + sections - 1
    first = section == 0
    final = section == sections - 1
    block_rows = hidden_in.shape[1]
    share = block_rows // lax.axis_size("mp")
    offset = lax.axis_index("mp") * share

    def project_all(normed):
        return (
            mixdot(normed, w_q).astype(jnp.bfloat16),
            mixdot(normed, w_k).astype(jnp.bfloat16),
            mixdot(normed, w_v).astype(jnp.bfloat16),
        )

    def attention_core(normed, slot_rows):
        query, key_tok, value_tok = project_all(normed)
        slot_normed, low_key, low_value, slot_keys, slot_values = slot_entries(
            slot_rows, gain, w_k, w_v, down_key, up_key, down_value, up_value
        )
        keys = jnp.concatenate([slot_keys, key_tok], axis=0)
        values = jnp.concatenate([slot_values, value_tok], axis=0)
        mixed, probs, weights = attend(query, keys, values)
        return (query, keys, values, mixed, probs, weights, slot_normed, low_key, low_value)

    arrive = jnp.zeros_like(hidden_in[0])
    kept_rows = jnp.zeros_like(hidden_in)
    for tick in range(ticks):
        micro = tick - section
        valid = (micro >= 0) & (micro < MICRO)
        place = jnp.clip(micro, 0, MICRO - 1)
        rows = jnp.where(first, hidden_in[min(tick, MICRO - 1)], arrive)
        kept_rows = jnp.where(
            valid, lax.dynamic_update_index_in_dim(kept_rows, rows, place, 0), kept_rows
        )
        unit, inverse = normalize(rows)
        normed = (unit * gain).astype(jnp.bfloat16)
        slot_rows = lax.dynamic_index_in_dim(slot_all, place, 0, keepdims=False)
        mixed = attention_core(normed, slot_rows)[3]
        summed = summed_on_arrival(mixdot(mixed, w_o), "mp", 0)
        own_rows = lax.dynamic_slice_in_dim(rows, offset, share, 0)
        own_result = (own_rows.astype(jnp.float32) + summed).astype(jnp.bfloat16)
        result = collect(own_result, "mp", 0)
        if tick + 1 < ticks:
            arrive = passed_along(result, "section", 1)
    grad_in = jnp.zeros((share, hidden_in.shape[2]), jnp.float32)
    sum_b = jnp.zeros((2,) + up_key.shape, jnp.float32)
    low_store = jnp.zeros((2, MICRO, SLOTS, up_key.shape[0]), jnp.float32)
    slot_store = jnp.zeros((MICRO, SLOTS, hidden_in.shape[2]), jnp.bfloat16)
    for tick in range(ticks):
        micro = tick - (sections - 1 - section)
        valid = (micro >= 0) & (micro < MICRO)
        place = jnp.clip(micro, 0, MICRO - 1)
        own_cot = lax.dynamic_slice_in_dim(cotangent[min(tick, MICRO - 1)], offset, share, 0)
        grad = jnp.where(final, own_cot.astype(jnp.float32), grad_in)
        rows = lax.dynamic_index_in_dim(kept_rows, place, 0, keepdims=False)
        unit, inverse = normalize(rows)
        normed = (unit * gain).astype(jnp.bfloat16)
        slot_rows = lax.dynamic_index_in_dim(slot_all, place, 0, keepdims=False)
        query, keys, values, mixed, probs, weights, slot_normed, low_key, low_value = (
            attention_core(normed, slot_rows)
        )
        grad_low = grad.astype(jnp.bfloat16)
        grad_mixed = mixdot(lax.all_gather(grad_low, "mp", axis=0, tiled=True), w_o.T).astype(
            jnp.bfloat16
        )
        grad_query, grad_keys, grad_values = attend_back(
            grad_mixed, query, keys, values, probs, weights
        )
        key_grad = grad_keys.astype(jnp.bfloat16)
        value_grad = grad_values.astype(jnp.bfloat16)
        total = mixdot(grad_query, w_q.T)
        total = total + mixdot(
            lax.dynamic_slice_in_dim(key_grad, SLOTS, share * lax.axis_size("mp"), 0), w_k.T
        )
        grad_normed = sent_and_summed(
            (
                total
                + mixdot(
                    lax.dynamic_slice_in_dim(value_grad, SLOTS, share * lax.axis_size("mp"), 0),
                    w_v.T,
                )
            ).astype(jnp.bfloat16),
            "mp",
            0,
        )
        own_unit = lax.dynamic_slice_in_dim(unit, offset, share, 0)
        own_inverse = lax.dynamic_slice_in_dim(inverse, offset, share, 0)
        scaled = grad_normed * gain
        grad_rows = grad + own_inverse * (
            scaled - own_unit * jnp.mean(scaled * own_unit, axis=-1, keepdims=True)
        )
        slot_key_grad = key_grad[:SLOTS]
        slot_value_grad = value_grad[:SLOTS]
        term_b = jnp.stack([mixdot(low_key.T, slot_key_grad), mixdot(low_value.T, slot_value_grad)])
        sum_b = sum_b + jnp.where(valid, term_b, 0.0)
        low_grads = jnp.stack(
            [mixdot(slot_key_grad, up_key.T), mixdot(slot_value_grad, up_value.T)]
        )
        low_store = jnp.where(
            valid, lax.dynamic_update_index_in_dim(low_store, low_grads, place, 1), low_store
        )
        slot_store = jnp.where(
            valid, lax.dynamic_update_index_in_dim(slot_store, slot_normed, place, 0), slot_store
        )
        if tick + 1 < ticks:
            grad_in = passed_along(grad_rows.astype(jnp.bfloat16), "section", -1).astype(
                grad_rows.dtype
            )
    low_total = taken_together(low_store, "mp")
    term = jnp.einsum("msd,tmsr->tdr", slot_store.astype(jnp.float32), low_total, precision=HIGH)
    grad_a, grad_b = (
        lax.psum(term.astype(jnp.bfloat16), "dp").astype(jnp.float32),
        lax.psum(sum_b.astype(jnp.bfloat16), "dp").astype(jnp.float32),
    )
    return (grad_a[None], grad_b[None])


def solution(mesh):
    placed = (
        P("dp", None, None),
        P("section", "dp", None, None),
        P("section", None),
        P("section", None, "mp"),
        P("section", None, "mp"),
        P("section", None, "mp"),
        P("section", "mp", None),
        P("section", None, None),
        P("section", None, "mp"),
        P("section", None, None),
        P("section", None, "mp"),
        P("dp", None, None),
    )
    return jax.shard_map(
        local,
        mesh=mesh,
        in_specs=placed,
        out_specs=(P("section", None, None, None), P("section", None, None, "mp")),
        check_vma=False,
    )
```

profile of v0, /device:TPU:0, one launch (start us, length us, event | category | flops | bytes accessed | tf_op | source)
XLA Modules:
  0.0 796.3 jit_solution(8733194437734446645)
XLA Ops:
  38.0 5.2 fusion.20
  43.2 5.6 all-to-all-start
  59.9 15.5 %all-to-all-done = f32[4,32,4096]{2,1,0:T(8,128)} async-done(((f32[4,32,4096]{2,1,0:T(8,128)}), f32[4,32,4096]{2,1,0:T(8,128)}, u32[]{:S(2)}, u32[]{:S(2)}) %all-to-all-start) | async-done | bytes 2097184 | tf_op jit(solution)/shard_map/all_to_all | solution.py:22
  80.2 4.3 all-to-all-start.1
  88.3 10.4 %all-to-all-done.1 = bf16[4,32,4096]{2,1,0:T(8,128)(2,1)} async-done(((bf16[4,32,4096]{2,1,0:T(8,128)(2,1)}), bf16[4,32,4096]{2,1,0:T(8,128)(2,1)}, u32[]{:S(2)}, u32[]{:S(2)}) %all-to-all-start.1) | async-done | bytes 1048608 | tf_op jit(solution)/shard_map/all_to_all | solution.py:34
  107.3 4.2 fusion.227
  117.4 5.1 fusion.18
  122.5 4.6 all-to-all-start.2
  133.0 15.4 %all-to-all-done.2 = f32[4,32,4096]{2,1,0:T(8,128)} async-done(((f32[4,32,4096]{2,1,0:T(8,128)}), f32[4,32,4096]{2,1,0:T(8,128)}, u32[]{:S(2)}, u32[]{:S(2)}) %all-to-all-start.2) | async-done | bytes 2097184 | tf_op jit(solution)/shard_map/all_to_all | solution.py:22
  152.3 4.4 all-to-all-start.3
  160.6 7.3 all-to-all-done.3
  167.9 7.3 collective-permute-start.1
  189.4 5.1 fusion.16
  194.6 4.6 all-to-all-start.4
  199.4 21.6 %all-to-all-done.4 = f32[4,32,4096]{2,1,0:T(8,128)} async-done(((f32[4,32,4096]{2,1,0:T(8,128)}), f32[4,32,4096]{2,1,0:T(8,128)}, u32[]{:S(2)}, u32[]{:S(2)}) %all-to-all-start.4) | async-done | bytes 2097184 | tf_op jit(solution)/shard_map/all_to_all | solution.py:22
  230.2 11.7 %all-to-all-done.5 = bf16[4,32,4096]{2,1,0:T(8,128)(2,1)} async-done(((bf16[4,32,4096]{2,1,0:T(8,128)(2,1)}), bf16[4,32,4096]{2,1,0:T(8,128)(2,1)}, u32[]{:S(2)}, u32[]{:S(2)}) %all-to-all-start.5) | async-done | bytes 1048608 | tf_op jit(solution)/shard_map/all_to_all | solution.py:34
  241.9 6.5 collective-permute-start.2
  252.6 4.9 fusion.233
  263.5 5.1 fusion.14
  268.5 4.7 all-to-all-start.6
  276.1 5.3 fusion.263
  282.2 10.2 %all-to-all-done.6 = f32[4,32,4096]{2,1,0:T(8,128)} async-done(((f32[4,32,4096]{2,1,0:T(8,128)}), f32[4,32,4096]{2,1,0:T(8,128)}, u32[]{:S(2)}, u32[]{:S(2)}) %all-to-all-start.6) | async-done | bytes 2097184 | tf_op jit(solution)/shard_map/all_to_all | solution.py:22
  304.0 8.5 %all-to-all-done.7 = bf16[4,32,4096]{2,1,0:T(8,128)(2,1)} async-done(((bf16[4,32,4096]{2,1,0:T(8,128)(2,1)}), bf16[4,32,4096]{2,1,0:T(8,128)(2,1)}, u32[]{:S(2)}, u32[]{:S(2)}) %all-to-all-start.7) | async-done | bytes 1048608 | tf_op jit(solution)/shard_map/all_to_all | solution.py:34
  312.5 9.2 %collective-permute-start.3 = (bf16[128,4096]{1,0:T(8,128)(2,1)}, bf16[128,4096]{1,0:T(8,128)(2,1)S(1)}, u32[]{:S(2)}, u32[]{:S(2)}) collective-permute-start(bf16[128,4096]{1,0:T(8,128)(2,1)} %bitcast.43), channel_id=1, source_target_pairs={{0,4},{4,8},{8,12},{1,5},{5,9},{9,13},{2,6},{6,10},{10,14},{3,7},{... | collective-permute-start | bytes 3145736 | tf_op jit(solution)/shard_map/ppermute | solution.py:44
  330.1 4.3 multiply_reduce_fusion
  345.5 6.3 fusion.44
  362.2 6.4 convert_bitcast_fusion
  376.5 7.7 collective-permute-done.4
  386.5 4.9 fusion.239
  403.7 12.3 %all-gather.8.cloned.1.call-done = bf16[128,4096]{1,0:T(8,128)(2,1)} async-done(((bf16[32,4096]{1,0:T(8,128)(2,1)}), bf16[128,4096]{1,0:T(8,128)(2,1)}) %all-gather.8.cloned.1.call-update) | async-done | bytes 1048592 | tf_op jit(solution)/shard_map/all_gather | solution.py:212
  416.0 6.0 fusion.251
  432.7 6.5 fusion.40
  448.8 4.4 all-to-all-start.9
  455.0 11.6 %all-to-all-done.9 = bf16[4,32,4096]{2,1,0:T(8,128)(2,1)} async-done(((bf16[4,32,4096]{2,1,0:T(8,128)(2,1)}), bf16[4,32,4096]{2,1,0:T(8,128)(2,1)}, u32[]{:S(2)}, u32[]{:S(2)}) %all-to-all-start.9) | async-done | bytes 1048608 | tf_op jit(solution)/shard_map/all_to_all | solution.py:49
  487.6 15.3 %all-gather.10.cloned.1.call-done = bf16[128,4096]{1,0:T(8,128)(2,1)} async-done(((bf16[32,4096]{1,0:T(8,128)(2,1)}), bf16[128,4096]{1,0:T(8,128)(2,1)}) %all-gather.10.cloned.1.call-update) | async-done | bytes 1048592 | tf_op jit(solution)/shard_map/all_gather | solution.py:212
  502.9 6.0 fusion.260
  518.7 6.4 fusion.36
  543.1 4.4 all-to-all-done.10
  560.8 4.8 fusion.248
  574.9 8.2 %all-gather.12.cloned.1.call-done = bf16[128,4096]{1,0:T(8,128)(2,1)} async-done(((bf16[32,4096]{1,0:T(8,128)(2,1)}), bf16[128,4096]{1,0:T(8,128)(2,1)}) %all-gather.12.cloned.1.call-update) | async-done | bytes 1048592 | tf_op jit(solution)/shard_map/all_gather | solution.py:212
  583.0 6.0 fusion.257
  599.7 6.4 fusion.32
  615.7 4.3 all-to-all-start.11
  628.6 4.8 all-to-all-done.11
  653.5 16.2 %all-gather.14.cloned.1.call-done = bf16[128,4096]{1,0:T(8,128)(2,1)} async-done(((bf16[32,4096]{1,0:T(8,128)(2,1)}), bf16[128,4096]{1,0:T(8,128)(2,1)}) %all-gather.14.cloned.1.call-update) | async-done | bytes 1048592 | tf_op jit(solution)/shard_map/all_gather | solution.py:212
  669.8 5.3 fusion.254
  686.6 4.9 all-to-all-done.12
  695.0 90.7 %all-reduce.3.cloned.1.call-done = (bf16[1,2,4096,64]{2,3,1,0:T(8,128)(2,1)}, bf16[1,2,64,256]{3,2,1,0:T(8,128)(2,1)}) async-done(((bf16[1,2,4096,64]{2,3,1,0:T(8,128)(2,1)}, bf16[1,2,64,256]{3,2,1,0:T(8,128)(2,1)}), (bf16[1,2,4096,64]{2,3,1,0:T(8,128)(2,1)}, bf16[1,2,64,256]{3,2,1,0:T(8,128)(2,1)})) %all-reduce.3.cloned.1.call-update) | async-done | bytes 1114128 | tf_op jit(solution)/shard_map/psum | solution.py:261
  (576 shorter events, 339.1 us)
Async XLA Ops:
  7.2 10.6 %copy-start = (bf16[1,4096,256]{2,1,0:T(8,128)(2,1)S(1)}, bf16[1,4096,256]{2,1,0:T(8,128)(2,1)}, u32[]{:S(2)}) copy-start(bf16[1,4096,256]{2,1,0:T(8,128)(2,1)} %param.16) | copy-start | bytes 6291460
  7.2 268.9 %all-gather.6.cloned.1.call-start = ((), (), s32[]{:S(2)}) async-start(), calls=%async_computation.13 | async-start | bytes 1310720 | tf_op jit(solution)/shard_map/all_gather | solution.py:212
  43.2 32.2 %all-to-all-start = ((f32[4,32,4096]{2,1,0:T(8,128)}), f32[4,32,4096]{2,1,0:T(8,128)}, u32[]{:S(2)}, u32[]{:S(2)}) async-start(f32[4,32,4096]{2,1,0:T(8,128)} %fusion.20), calls=%async_computation | async-start | bytes 4194304 | tf_op jit(solution)/shard_map/all_to_all | solution.py:22
  80.2 18.5 %all-to-all-start.1 = ((bf16[4,32,4096]{2,1,0:T(8,128)(2,1)}), bf16[4,32,4096]{2,1,0:T(8,128)(2,1)}, u32[]{:S(2)}, u32[]{:S(2)}) async-start(bf16[4,32,4096]{2,1,0:T(8,128)(2,1)} %broadcast_in_dim.174), calls=%async_computation.1 | async-start | bytes 2097152 | tf_op jit(solution)/shard_map/all_to_all | solution.py:34
  86.5 18.2 %copy-start.54 = (f32[16,256]{1,0:T(8,128)S(1)}, f32[16,256]{1,0:T(8,128)}, u32[]{:S(2)}) copy-start(f32[16,256]{1,0:T(8,128)} %fusion.458) | copy-start | bytes 49156
  86.5 18.2 %copy-start.107 = (f32[16]{0:T(128)S(1)}, f32[16]{0:T(128)}, u32[]{:S(2)}) copy-start(f32[16]{0:T(128)} %copy-done.106) | copy-start | bytes 196
  98.7 8.1 %collective-permute-start = (bf16[128,4096]{1,0:T(8,128)(2,1)}, bf16[128,4096]{1,0:T(8,128)(2,1)S(1)}, u32[]{:S(2)}, u32[]{:S(2)}) collective-permute-start(bf16[128,4096]{1,0:T(8,128)(2,1)} %bitcast.19), channel_id=1, source_target_pairs={{0,4},{4,8},{8,12},{1,5},{5,9},{9,13},{2,6},{6,10},{10,14},{3,7},{... | collective-permute-start | bytes 3145736 | tf_op jit(solution)/shard_map/ppermute | solution.py:44
  122.5 25.9 %all-to-all-start.2 = ((f32[4,32,4096]{2,1,0:T(8,128)}), f32[4,32,4096]{2,1,0:T(8,128)}, u32[]{:S(2)}, u32[]{:S(2)}) async-start(f32[4,32,4096]{2,1,0:T(8,128)} %fusion.18), calls=%async_computation.2 | async-start | bytes 4194304 | tf_op jit(solution)/shard_map/all_to_all | solution.py:22
  152.3 7.3 copy-start.59
  152.3 7.3 copy-start.91
  152.3 15.6 %all-to-all-start.3 = ((bf16[4,32,4096]{2,1,0:T(8,128)(2,1)}), bf16[4,32,4096]{2,1,0:T(8,128)(2,1)}, u32[]{:S(2)}, u32[]{:S(2)}) async-start(bf16[4,32,4096]{2,1,0:T(8,128)(2,1)} %broadcast_in_dim.176), calls=%async_computation.3 | async-start | bytes 2097152 | tf_op jit(solution)/shard_map/all_to_all | solution.py:34
  156.9 18.3 %copy-start.64 = (bf16[16,64]{1,0:T(8,128)(2,1)S(1)}, bf16[16,64]{1,0:T(8,128)(2,1)}, u32[]{:S(2)}) copy-start(bf16[16,64]{1,0:T(8,128)(2,1)} %convolution_convert_fusion.10) | copy-start | bytes 6148
  159.6 18.5 %copy-start.94 = (f32[16]{0:T(128)S(1)}, f32[16]{0:T(128)}, u32[]{:S(2)}) copy-start(f32[16]{0:T(128)} %copy-done.93) | copy-start | bytes 196
  167.9 12.3 %collective-permute-start.1 = (bf16[128,4096]{1,0:T(8,128)(2,1)}, bf16[128,4096]{1,0:T(8,128)(2,1)S(1)}, u32[]{:S(2)}, u32[]{:S(2)}) collective-permute-start(bf16[128,4096]{1,0:T(8,128)(2,1)} %bitcast.27), channel_id=1, source_target_pairs={{0,4},{4,8},{8,12},{1,5},{5,9},{9,13},{2,6},{6,10},{10,14},{3,7},{... | collective-permute-start | bytes 3145736 | tf_op jit(solution)/shard_map/ppermute | solution.py:44
  194.6 26.5 %all-to-all-start.4 = ((f32[4,32,4096]{2,1,0:T(8,128)}), f32[4,32,4096]{2,1,0:T(8,128)}, u32[]{:S(2)}, u32[]{:S(2)}) async-start(f32[4,32,4096]{2,1,0:T(8,128)} %fusion.16), calls=%async_computation.4 | async-start | bytes 4194304 | tf_op jit(solution)/shard_map/all_to_all | solution.py:22
  224.8 23.7 %copy-start.87 = (f32[16]{0:T(128)S(1)}, f32[16]{0:T(128)}, u32[]{:S(2)}) copy-start(f32[16]{0:T(128)} %copy-done.86) | copy-start | bytes 196
  224.8 24.6 %copy-start.95 = (f32[16]{0:T(128)S(1)}, f32[16]{0:T(128)}, u32[]{:S(2)}) copy-start(f32[16]{0:T(128)} %copy-done.93) | copy-start | bytes 196
  225.9 16.1 %all-to-all-start.5 = ((bf16[4,32,4096]{2,1,0:T(8,128)(2,1)}), bf16[4,32,4096]{2,1,0:T(8,128)(2,1)}, u32[]{:S(2)}, u32[]{:S(2)}) async-start(bf16[4,32,4096]{2,1,0:T(8,128)(2,1)} %broadcast_in_dim.178), calls=%async_computation.5 | async-start | bytes 2097152 | tf_op jit(solution)/shard_map/all_to_all | solution.py:34
  241.9 8.9 %collective-permute-start.2 = (bf16[128,4096]{1,0:T(8,128)(2,1)}, bf16[128,4096]{1,0:T(8,128)(2,1)S(1)}, u32[]{:S(2)}, u32[]{:S(2)}) collective-permute-start(bf16[128,4096]{1,0:T(8,128)(2,1)} %bitcast.35), channel_id=1, source_target_pairs={{0,4},{4,8},{8,12},{1,5},{5,9},{9,13},{2,6},{6,10},{10,14},{3,7},{... | collective-permute-start | bytes 3145736 | tf_op jit(solution)/shard_map/ppermute | solution.py:44
  268.5 23.8 %all-to-all-start.6 = ((f32[4,32,4096]{2,1,0:T(8,128)}), f32[4,32,4096]{2,1,0:T(8,128)}, u32[]{:S(2)}, u32[]{:S(2)}) async-start(f32[4,32,4096]{2,1,0:T(8,128)} %fusion.14), calls=%async_computation.6 | async-start | bytes 4194304 | tf_op jit(solution)/shard_map/all_to_all | solution.py:22
  297.3 15.2 %all-to-all-start.7 = ((bf16[4,32,4096]{2,1,0:T(8,128)(2,1)}), bf16[4,32,4096]{2,1,0:T(8,128)(2,1)}, u32[]{:S(2)}, u32[]{:S(2)}) async-start(bf16[4,32,4096]{2,1,0:T(8,128)(2,1)} %broadcast_in_dim.180), calls=%async_computation.7 | async-start | bytes 2097152 | tf_op jit(solution)/shard_map/all_to_all | solution.py:34
  304.0 20.7 %copy-start.26 = (bf16[128,4096]{1,0:T(8,128)(2,1)S(1)}, bf16[128,4096]{1,0:T(8,128)(2,1)}, u32[]{:S(2)}) copy-start(bf16[128,4096]{1,0:T(8,128)(2,1)} %copy-done.25) | copy-start | bytes 3145732
  312.5 14.8 %collective-permute-start.3 = (bf16[128,4096]{1,0:T(8,128)(2,1)}, bf16[128,4096]{1,0:T(8,128)(2,1)S(1)}, u32[]{:S(2)}, u32[]{:S(2)}) collective-permute-start(bf16[128,4096]{1,0:T(8,128)(2,1)} %bitcast.43), channel_id=1, source_target_pairs={{0,4},{4,8},{8,12},{1,5},{5,9},{9,13},{2,6},{6,10},{10,14},{3,7},{... | collective-permute-start | bytes 3145736 | tf_op jit(solution)/shard_map/ppermute | solution.py:44
  324.7 9.7 %slice-start = ((s8[6291456]{0:T(1024)(128)(4,1)}), s8[4194304]{0:T(1024)(128)(4,1)S(1)}, s32[]{:S(2)}) async-start(s8[6291456]{0:T(1024)(128)(4,1)} %bitcast.1136), calls=%async_computation.19 | async-start | bytes 8388608
  342.3 9.7 %copy-start.47 = (bf16[144,2,128]{2,0,1:T(8,128)(2,1)}, bf16[144,2,128]{2,0,1:T(8,128)(2,1)S(1)}, u32[]{:S(2)}) copy-start(bf16[144,2,128]{2,0,1:T(8,128)(2,1)S(1)} %fusion.343) | copy-start | bytes 221188
  344.0 7.9 copy-start.46
  356.6 14.4 %all-to-all-start.8 = ((bf16[4,32,4096]{2,1,0:T(8,128)(2,1)}), bf16[4,32,4096]{2,1,0:T(8,128)(2,1)S(1)}, u32[]{:S(2)}, u32[]{:S(2)}) async-start(bf16[4,32,4096]{2,1,0:T(8,128)(2,1)} %bitcast.1216), calls=%async_computation.8 | async-start | bytes 2097152 | tf_op jit(solution)/shard_map/all_to_all | solution.py:49
  360.1 55.9 %all-gather.8.cloned.1.call-start = ((), (), s32[]{:S(2)}) async-start(), calls=%async_computation.14 | async-start | bytes 1310720 | tf_op jit(solution)/shard_map/all_gather | solution.py:212
  372.4 12.6 %copy-start.19 = (bf16[1,128,4096]{2,1,0:T(8,128)(2,1)S(1)}, bf16[1,128,4096]{2,1,0:T(8,128)(2,1)}, u32[]{:S(2)}) copy-start(bf16[1,128,4096]{2,1,0:T(8,128)(2,1)} %get-tuple-element.29) | copy-start | bytes 3145732
  373.8 10.5 %collective-permute-start.4 = (bf16[32,4096]{1,0:T(8,128)(2,1)S(1)}, bf16[32,4096]{1,0:T(8,128)(2,1)S(1)}, u32[]{:S(2)}, u32[]{:S(2)}) collective-permute-start(bf16[32,4096]{1,0:T(8,128)(2,1)S(1)} %fusion.489), channel_id=1, source_target_pairs={{4,0},{8,4},{12,8},{5,1},{9,5},{13,9},{6,2},{10,6},{14,10},{7,3},{... | collective-permute-start | bytes 786440 | tf_op jit(solution)/shard_map/ppermute | solution.py:44
  448.8 17.8 %all-to-all-start.9 = ((bf16[4,32,4096]{2,1,0:T(8,128)(2,1)}), bf16[4,32,4096]{2,1,0:T(8,128)(2,1)}, u32[]{:S(2)}, u32[]{:S(2)}) async-start(bf16[4,32,4096]{2,1,0:T(8,128)(2,1)} %bitcast.1217), calls=%async_computation.9 | async-start | bytes 2097152 | tf_op jit(solution)/shard_map/all_to_all | solution.py:49
  453.2 49.7 %all-gather.10.cloned.1.call-start = ((), (), s32[]{:S(2)}) async-start(), calls=%async_computation.15 | async-start | bytes 1310720 | tf_op jit(solution)/shard_map/all_gather | solution.py:212
  470.7 3.4 collective-permute-start.5
  529.9 17.6 %all-to-all-start.10 = ((bf16[4,32,4096]{2,1,0:T(8,128)(2,1)}), bf16[4,32,4096]{2,1,0:T(8,128)(2,1)}, u32[]{:S(2)}, u32[]{:S(2)}) async-start(bf16[4,32,4096]{2,1,0:T(8,128)(2,1)} %bitcast.1215), calls=%async_computation.10 | async-start | bytes 2097152 | tf_op jit(solution)/shard_map/all_to_all | solution.py:49
  534.1 48.9 %all-gather.12.cloned.1.call-start = ((), (), s32[]{:S(2)}) async-start(), calls=%async_computation.16 | async-start | bytes 1310720 | tf_op jit(solution)/shard_map/all_gather | solution.py:212
  540.9 9.4 %copy-start.33 = (bf16[32,4096]{1,0:T(8,128)(2,1)S(1)}, bf16[32,4096]{1,0:T(8,128)(2,1)}, u32[]{:S(2)}) copy-start(bf16[32,4096]{1,0:T(8,128)(2,1)} %copy-done.32) | copy-start | bytes 786436
  551.6 3.9 collective-permute-start.6
  615.7 17.6 %all-to-all-start.11 = ((bf16[4,32,4096]{2,1,0:T(8,128)(2,1)}), bf16[4,32,4096]{2,1,0:T(8,128)(2,1)}, u32[]{:S(2)}, u32[]{:S(2)}) async-start(bf16[4,32,4096]{2,1,0:T(8,128)(2,1)} %bitcast.1214), calls=%async_computation.11 | async-start | bytes 2097152 | tf_op jit(solution)/shard_map/all_to_all | solution.py:49
  620.0 49.8 %all-gather.14.cloned.1.call-start = ((), (), s32[]{:S(2)}) async-start(), calls=%async_computation.17 | async-start | bytes 1310720 | tf_op jit(solution)/shard_map/all_gather | solution.py:212
  638.0 5.2 collective-permute-start.7
  653.5 21.8 %copy-start.45 = (bf16[128,768]{0,1:T(8,128)(2,1)S(1)}, bf16[128,768]{0,1:T(8,128)(2,1)}, u32[]{:S(2)}) copy-start(bf16[128,768]{0,1:T(8,128)(2,1)} %copy.220) | copy-start | bytes 589828
  653.5 21.8 %copy-start.119 = (f32[2,3,128]{2,1,0:T(4,128)S(1)}, f32[2,3,128]{2,1,0:T(4,128)}, u32[]{:S(2)}) copy-start(f32[2,3,128]{2,1,0:T(4,128)} %get-tuple-element.39) | copy-start | bytes 9220
  676.6 9.3 %copy-start.40 = (f32[1,64,256]{2,1,0:T(8,128)S(1)}, f32[1,64,256]{2,1,0:T(8,128)}, u32[]{:S(2)}) copy-start(f32[1,64,256]{2,1,0:T(8,128)} %convolution_bitcast_fusion.23) | copy-start | bytes 196612
  676.6 9.3 %copy-start.41 = (f32[1,64,256]{2,1,0:T(8,128)S(1)}, f32[1,64,256]{2,1,0:T(8,128)}, u32[]{:S(2)}) copy-start(f32[1,64,256]{2,1,0:T(8,128)} %convolution_bitcast_fusion.24) | copy-start | bytes 196612
  677.8 8.1 %copy-start.42 = (f32[1,64,256]{2,1,0:T(8,128)S(1)}, f32[1,64,256]{2,1,0:T(8,128)}, u32[]{:S(2)}) copy-start(f32[1,64,256]{2,1,0:T(8,128)} %convolution_bitcast_fusion.15) | copy-start | bytes 196612
  677.8 15.2 %copy-start.30 = (bf16[2,16,4096]{2,1,0:T(8,128)(2,1)S(1)}, bf16[2,16,4096]{2,1,0:T(8,128)(2,1)}, u32[]{:S(2)}) copy-start(bf16[2,16,4096]{2,1,0:T(8,128)(2,1)} %fusion.579) | copy-start | bytes 786436
  682.6 9.0 %all-to-all-start.12 = ((f32[4,1,4096]{2,1,0:T(1,128)}), f32[4,1,4096]{2,1,0:T(1,128)S(1)}, u32[]{:S(2)}, u32[]{:S(2)}) async-start(f32[4,1,4096]{2,1,0:T(1,128)} %reshape.1693), calls=%async_computation.12 | async-start | bytes 131072 | tf_op jit(solution)/shard_map/all_to_all | solution.py:34
  685.9 99.8 %all-reduce.3.cloned.1.call-start = ((), (), s32[]{:S(2)}) async-start(), calls=%async_computation.18 | async-start | bytes 2228224 | tf_op jit(solution)/shard_map/psum | solution.py:261
  (102 other events, 378.7 us)
Sparse Core Ops, SparseCore 0:
  11.1 26.8 all-gather.5
  385.9 30.0 all-gather.7
  475.8 27.0 all-gather.9
  556.4 26.6 all-gather.11
  644.2 25.5 all-gather.13
  695.2 90.5 all-reduce.2
where the time goes:
time: 808 us; the launch traced here: 796 us
  waiting for transfers between devices  281 us (35%)
  matrix products  277 us (34%)
  starting transfers between devices  87.2 us (11%)
  other arithmetic  78.6 us (10%)
  local copies, waits for them, and re-layouts  56.6 us (7%)
  between operations  16.3 us (2%)
    dot_general x114, matrix products, mixdot(): return jnp.dot(left, right, preferred_element_type=jnp.float32)  220 us
    psum x1, waiting for transfers between devices, local(): lax.psum(term.astype(jnp.bfloat16), 'dp').astype(jnp.float32)  90.7 us
    all_to_all x4, waiting for transfers between devices, summed_on_arrival(): lax.all_to_all(in_blocks(array, dim, length), axis, 0, 0, tiled=True)  62.7 us
    all_gather x5, waiting for transfers between devices, local(): lax.all_gather(grad_low, 'mp', axis=0, tiled=True)  52.1 us
    all_to_all x5, waiting for transfers between devices, copy_for_each(): return lax.all_to_all(copies, axis, split_axis=0, concat_axis=0, tiled=True)  42.8 us
    ppermute x8, starting transfers between devices, passed_along(): return lax.ppermute(block, axis, route)  30.8 us
    all_to_all x4, waiting for transfers between devices, sent_and_summed(): lax.all_to_all(pieces, axis, split_axis=0, concat_axis=0, tiled=True)  23 us
    all_to_all x5, starting transfers between devices, copy_for_each(): return lax.all_to_all(copies, axis, split_axis=0, concat_axis=0, tiled=True)  20.5 us
  transfers between devices with their start and end apart: 27, of which 21 were waited for; matrix products, arithmetic and copies ran while one was open for 30% of the time, Pallas kernels for 0%

commit v1 on v0

--- a/solution.py
+++ b/solution.py
@@ -258,7 +258,7 @@
     low_total = taken_together(low_store, "mp")
     term = jnp.einsum("msd,tmsr->tdr", slot_store.astype(jnp.float32), low_total, precision=HIGH)
     grad_a, grad_b = (
-        lax.psum(term.astype(jnp.bfloat16), "dp").astype(jnp.float32),
+        jnp.sum(lax.all_gather(term.astype(jnp.bfloat16), "dp"), axis=0).astype(jnp.float32),
         lax.psum(sum_b.astype(jnp.bfloat16), "dp").astype(jnp.float32),
     )
     return (grad_a[None], grad_b[None])

time: 808 us -> 907 us (1.12)
  waiting for transfers between devices: 281 us -> 377 us
    all_gather x0 -> x1, waiting for transfers between devices: none -> 106 us  [local(): lax.all_gather(term.astype(jnp.bfloat16), 'dp')]
    psum x1, waiting for transfers between devices: 90.7 us -> 79.7 us  [local(): lax.psum(sum_b.astype(jnp.bfloat16), 'dp').astype(jnp.float32)]
  transfers between devices with their start and end apart: 27 -> 28, of which waited for: 21 -> 22; matrix products, arithmetic and copies ran while one was open for 30% -> 27% of each run, Pallas kernels for 0% -> 0%
where the time goes in v1:
time: 907 us; the launch traced here: 895 us
  waiting for transfers between devices  377 us (42%)
  matrix products  275 us (30%)
  starting transfers between devices  87.6 us (10%)
  other arithmetic  83.2 us (9%)
  local copies, waits for them, and re-layouts  56.5 us (6%)
  between operations  16.3 us (2%)
    dot_general x114, matrix products, mixdot(): return jnp.dot(left, right, preferred_element_type=jnp.float32)  218 us
    all_gather x1, waiting for transfers between devices, local(): lax.all_gather(term.astype(jnp.bfloat16), 'dp')  106 us
    psum x1, waiting for transfers between devices, local(): lax.psum(sum_b.astype(jnp.bfloat16), 'dp').astype(jnp.float32)  79.7 us
    all_to_all x4, waiting for transfers between devices, summed_on_arrival(): lax.all_to_all(in_blocks(array, dim, length), axis, 0, 0, tiled=True)  62.8 us
    all_gather x5, waiting for transfers between devices, local(): lax.all_gather(grad_low, 'mp', axis=0, tiled=True)  52.7 us
    all_to_all x5, waiting for transfers between devices, copy_for_each(): return lax.all_to_all(copies, axis, split_axis=0, concat_axis=0, tiled=True)  42.7 us
    ppermute x8, starting transfers between devices, passed_along(): return lax.ppermute(block, axis, route)  30.8 us
    all_to_all x4, waiting for transfers between devices, sent_and_summed(): lax.all_to_all(pieces, axis, split_axis=0, concat_axis=0, tiled=True)  23 us
  transfers between devices with their start and end apart: 28, of which 22 were waited for; matrix products, arithmetic and copies ran while one was open for 27% of the time, Pallas kernels for 0%

profile of v1, /device:TPU:0, one launch (start us, length us, event | category | flops | bytes accessed | tf_op | source)
XLA Modules:
  0.0 895.2 jit_solution(9779160843662902121)
XLA Ops:
  13.7 4.5 fusion.224
  40.3 5.2 fusion.20
  45.5 5.6 all-to-all-start
  62.2 15.5 %all-to-all-done = f32[4,32,4096]{2,1,0:T(8,128)} async-done(((f32[4,32,4096]{2,1,0:T(8,128)}), f32[4,32,4096]{2,1,0:T(8,128)}, u32[]{:S(2)}, u32[]{:S(2)}) %all-to-all-start) | async-done | bytes 2097184 | tf_op jit(solution)/shard_map/all_to_all | solution.py:22
  90.5 10.4 %all-to-all-done.1 = bf16[4,32,4096]{2,1,0:T(8,128)(2,1)} async-done(((bf16[4,32,4096]{2,1,0:T(8,128)(2,1)}), bf16[4,32,4096]{2,1,0:T(8,128)(2,1)}, u32[]{:S(2)}, u32[]{:S(2)}) %all-to-all-start.1) | async-done | bytes 1048608 | tf_op jit(solution)/shard_map/all_to_all | solution.py:34
  119.7 5.1 fusion.18
  124.8 4.6 all-to-all-start.2
  135.3 15.5 %all-to-all-done.2 = f32[4,32,4096]{2,1,0:T(8,128)} async-done(((f32[4,32,4096]{2,1,0:T(8,128)}), f32[4,32,4096]{2,1,0:T(8,128)}, u32[]{:S(2)}, u32[]{:S(2)}) %all-to-all-start.2) | async-done | bytes 2097184 | tf_op jit(solution)/shard_map/all_to_all | solution.py:22
  154.6 4.4 all-to-all-start.3
  162.9 7.3 all-to-all-done.3
  170.2 7.3 collective-permute-start.1
  191.7 5.1 fusion.16
  196.9 4.6 all-to-all-start.4
  201.7 21.6 %all-to-all-done.4 = f32[4,32,4096]{2,1,0:T(8,128)} async-done(((f32[4,32,4096]{2,1,0:T(8,128)}), f32[4,32,4096]{2,1,0:T(8,128)}, u32[]{:S(2)}, u32[]{:S(2)}) %all-to-all-start.4) | async-done | bytes 2097184 | tf_op jit(solution)/shard_map/all_to_all | solution.py:22
  232.5 11.7 %all-to-all-done.5 = bf16[4,32,4096]{2,1,0:T(8,128)(2,1)} async-done(((bf16[4,32,4096]{2,1,0:T(8,128)(2,1)}), bf16[4,32,4096]{2,1,0:T(8,128)(2,1)}, u32[]{:S(2)}, u32[]{:S(2)}) %all-to-all-start.5) | async-done | bytes 1048608 | tf_op jit(solution)/shard_map/all_to_all | solution.py:34
  244.2 6.5 collective-permute-start.2
  262.8 5.1 fusion.14
  267.8 4.7 all-to-all-start.6
  275.4 5.3 fusion.263
  281.5 10.2 %all-to-all-done.6 = f32[4,32,4096]{2,1,0:T(8,128)} async-done(((f32[4,32,4096]{2,1,0:T(8,128)}), f32[4,32,4096]{2,1,0:T(8,128)}, u32[]{:S(2)}, u32[]{:S(2)}) %all-to-all-start.6) | async-done | bytes 2097184 | tf_op jit(solution)/shard_map/all_to_all | solution.py:22
  303.3 8.5 all-to-all-done.7
  311.8 9.2 %collective-permute-start.3 = (bf16[128,4096]{1,0:T(8,128)(2,1)}, bf16[128,4096]{1,0:T(8,128)(2,1)S(1)}, u32[]{:S(2)}, u32[]{:S(2)}) collective-permute-start(bf16[128,4096]{1,0:T(8,128)(2,1)} %bitcast.43), channel_id=1, source_target_pairs={{0,4},{4,8},{8,12},{1,5},{5,9},{9,13},{2,6},{6,10},{10,14},{3,7},{... | collective-permute-start | bytes 3145736 | tf_op jit(solution)/shard_map/ppermute | solution.py:44
  329.4 4.3 multiply_reduce_fusion
  344.9 6.3 fusion.44
  361.5 6.4 convert_bitcast_fusion
  375.8 7.8 collective-permute-done.4
  385.8 4.9 fusion.239
  403.0 12.2 %all-gather.10.cloned.1.call-done = bf16[128,4096]{1,0:T(8,128)(2,1)} async-done(((bf16[32,4096]{1,0:T(8,128)(2,1)}), bf16[128,4096]{1,0:T(8,128)(2,1)}) %all-gather.10.cloned.1.call-update) | async-done | bytes 1048592 | tf_op jit(solution)/shard_map/all_gather | solution.py:212
  415.1 6.0 fusion.251
  431.8 6.5 fusion.40
  447.9 4.4 all-to-all-start.9
  454.1 11.5 %all-to-all-done.9 = bf16[4,32,4096]{2,1,0:T(8,128)(2,1)} async-done(((bf16[4,32,4096]{2,1,0:T(8,128)(2,1)}), bf16[4,32,4096]{2,1,0:T(8,128)(2,1)}, u32[]{:S(2)}, u32[]{:S(2)}) %all-to-all-start.9) | async-done | bytes 1048608 | tf_op jit(solution)/shard_map/all_to_all | solution.py:49
  486.7 15.4 %all-gather.12.cloned.1.call-done = bf16[128,4096]{1,0:T(8,128)(2,1)} async-done(((bf16[32,4096]{1,0:T(8,128)(2,1)}), bf16[128,4096]{1,0:T(8,128)(2,1)}) %all-gather.12.cloned.1.call-update) | async-done | bytes 1048592 | tf_op jit(solution)/shard_map/all_gather | solution.py:212
  502.1 6.0 fusion.260
  517.9 6.4 fusion.36
  542.3 4.4 all-to-all-done.10
  560.0 4.8 fusion.248
  574.0 8.2 all-gather.14.cloned.1.call-done
  582.2 6.0 fusion.257
  598.9 6.4 fusion.32
  614.9 4.3 all-to-all-start.11
  627.8 4.8 all-to-all-done.11
  653.0 17.0 %all-gather.16.cloned.1.call-done = bf16[128,4096]{1,0:T(8,128)(2,1)} async-done(((bf16[32,4096]{1,0:T(8,128)(2,1)}), bf16[128,4096]{1,0:T(8,128)(2,1)}) %all-gather.16.cloned.1.call-update) | async-done | bytes 1048592 | tf_op jit(solution)/shard_map/all_gather | solution.py:212
  670.0 5.3 fusion.254
  686.6 4.8 all-to-all-done.12
  694.9 79.7 %all-reduce.2.cloned.1.call-done = bf16[1,2,64,256]{3,2,1,0:T(8,128)(2,1)} async-done(((bf16[1,2,64,256]{3,2,1,0:T(8,128)(2,1)}), bf16[1,2,64,256]{3,2,1,0:T(8,128)(2,1)}) %all-reduce.2.cloned.1.call-update) | async-done | bytes 65552 | tf_op jit(solution)/shard_map/psum | solution.py:262
  776.1 105.5 %all-gather.18.cloned.1.call-done = bf16[16,4096,64]{1,2,0:T(8,128)(2,1)} async-done(((bf16[2,4096,64]{1,2,0:T(8,128)(2,1)}), bf16[16,4096,64]{1,2,0:T(8,128)(2,1)}) %all-gather.18.cloned.1.call-update) | async-done | bytes 8388624 | tf_op jit(solution)/shard_map/all_gather | solution.py:261
  881.6 4.9 reduce_sum.462
  (572 shorter events, 346.8 us)
Async XLA Ops:
  7.2 12.9 %copy-start = (bf16[1,4096,256]{2,1,0:T(8,128)(2,1)S(1)}, bf16[1,4096,256]{2,1,0:T(8,128)(2,1)}, u32[]{:S(2)}) copy-start(bf16[1,4096,256]{2,1,0:T(8,128)(2,1)} %param.16) | copy-start | bytes 6291460
  7.2 268.2 %all-gather.8.cloned.1.call-start = ((), (), s32[]{:S(2)}) async-start(), calls=%async_computation.13 | async-start | bytes 1310720 | tf_op jit(solution)/shard_map/all_gather | solution.py:212
  10.2 8.1 copy-start.31
  45.5 32.2 %all-to-all-start = ((f32[4,32,4096]{2,1,0:T(8,128)}), f32[4,32,4096]{2,1,0:T(8,128)}, u32[]{:S(2)}, u32[]{:S(2)}) async-start(f32[4,32,4096]{2,1,0:T(8,128)} %fusion.20), calls=%async_computation | async-start | bytes 4194304 | tf_op jit(solution)/shard_map/all_to_all | solution.py:22
  82.5 18.5 %all-to-all-start.1 = ((bf16[4,32,4096]{2,1,0:T(8,128)(2,1)}), bf16[4,32,4096]{2,1,0:T(8,128)(2,1)}, u32[]{:S(2)}, u32[]{:S(2)}) async-start(bf16[4,32,4096]{2,1,0:T(8,128)(2,1)} %broadcast_in_dim.169), calls=%async_computation.1 | async-start | bytes 2097152 | tf_op jit(solution)/shard_map/all_to_all | solution.py:34
  88.7 18.2 %copy-start.52 = (f32[16,256]{1,0:T(8,128)S(1)}, f32[16,256]{1,0:T(8,128)}, u32[]{:S(2)}) copy-start(f32[16,256]{1,0:T(8,128)} %fusion.458) | copy-start | bytes 49156
  88.7 18.2 %copy-start.103 = (f32[16]{0:T(128)S(1)}, f32[16]{0:T(128)}, u32[]{:S(2)}) copy-start(f32[16]{0:T(128)} %copy-done.102) | copy-start | bytes 196
  100.9 8.1 collective-permute-start
  124.8 25.9 %all-to-all-start.2 = ((f32[4,32,4096]{2,1,0:T(8,128)}), f32[4,32,4096]{2,1,0:T(8,128)}, u32[]{:S(2)}, u32[]{:S(2)}) async-start(f32[4,32,4096]{2,1,0:T(8,128)} %fusion.18), calls=%async_computation.2 | async-start | bytes 4194304 | tf_op jit(solution)/shard_map/all_to_all | solution.py:22
  154.6 15.7 %all-to-all-start.3 = ((bf16[4,32,4096]{2,1,0:T(8,128)(2,1)}), bf16[4,32,4096]{2,1,0:T(8,128)(2,1)}, u32[]{:S(2)}, u32[]{:S(2)}) async-start(bf16[4,32,4096]{2,1,0:T(8,128)(2,1)} %broadcast_in_dim.171), calls=%async_computation.3 | async-start | bytes 2097152 | tf_op jit(solution)/shard_map/all_to_all | solution.py:34
  159.2 18.3 %copy-start.60 = (bf16[16,64]{1,0:T(8,128)(2,1)S(1)}, bf16[16,64]{1,0:T(8,128)(2,1)}, u32[]{:S(2)}) copy-start(bf16[16,64]{1,0:T(8,128)(2,1)} %convolution_convert_fusion.10) | copy-start | bytes 6148
  161.9 18.5 %copy-start.90 = (f32[16]{0:T(128)S(1)}, f32[16]{0:T(128)}, u32[]{:S(2)}) copy-start(f32[16]{0:T(128)} %copy-done.89) | copy-start | bytes 196
  170.2 12.2 %collective-permute-start.1 = (bf16[128,4096]{1,0:T(8,128)(2,1)}, bf16[128,4096]{1,0:T(8,128)(2,1)S(1)}, u32[]{:S(2)}, u32[]{:S(2)}) collective-permute-start(bf16[128,4096]{1,0:T(8,128)(2,1)} %bitcast.27), channel_id=1, source_target_pairs={{0,4},{4,8},{8,12},{1,5},{5,9},{9,13},{2,6},{6,10},{10,14},{3,7},{... | collective-permute-start | bytes 3145736 | tf_op jit(solution)/shard_map/ppermute | solution.py:44
  196.9 26.5 %all-to-all-start.4 = ((f32[4,32,4096]{2,1,0:T(8,128)}), f32[4,32,4096]{2,1,0:T(8,128)}, u32[]{:S(2)}, u32[]{:S(2)}) async-start(f32[4,32,4096]{2,1,0:T(8,128)} %fusion.16), calls=%async_computation.4 | async-start | bytes 4194304 | tf_op jit(solution)/shard_map/all_to_all | solution.py:22
  227.1 23.7 %copy-start.83 = (f32[16]{0:T(128)S(1)}, f32[16]{0:T(128)}, u32[]{:S(2)}) copy-start(f32[16]{0:T(128)} %copy-done.82) | copy-start | bytes 196
  227.1 24.6 %copy-start.91 = (f32[16]{0:T(128)S(1)}, f32[16]{0:T(128)}, u32[]{:S(2)}) copy-start(f32[16]{0:T(128)} %copy-done.89) | copy-start | bytes 196
  228.2 16.1 %all-to-all-start.5 = ((bf16[4,32,4096]{2,1,0:T(8,128)(2,1)}), bf16[4,32,4096]{2,1,0:T(8,128)(2,1)}, u32[]{:S(2)}, u32[]{:S(2)}) async-start(bf16[4,32,4096]{2,1,0:T(8,128)(2,1)} %broadcast_in_dim.173), calls=%async_computation.5 | async-start | bytes 2097152 | tf_op jit(solution)/shard_map/all_to_all | solution.py:34
  244.2 8.9 collective-permute-start.2
  251.8 7.3 copy-start.29
  267.8 23.9 %all-to-all-start.6 = ((f32[4,32,4096]{2,1,0:T(8,128)}), f32[4,32,4096]{2,1,0:T(8,128)}, u32[]{:S(2)}, u32[]{:S(2)}) async-start(f32[4,32,4096]{2,1,0:T(8,128)} %fusion.14), calls=%async_computation.6 | async-start | bytes 4194304 | tf_op jit(solution)/shard_map/all_to_all | solution.py:22
  296.6 15.2 %all-to-all-start.7 = ((bf16[4,32,4096]{2,1,0:T(8,128)(2,1)}), bf16[4,32,4096]{2,1,0:T(8,128)(2,1)}, u32[]{:S(2)}, u32[]{:S(2)}) async-start(bf16[4,32,4096]{2,1,0:T(8,128)(2,1)} %broadcast_in_dim.175), calls=%async_computation.7 | async-start | bytes 2097152 | tf_op jit(solution)/shard_map/all_to_all | solution.py:34
  303.3 20.6 %copy-start.26 = (bf16[128,4096]{1,0:T(8,128)(2,1)S(1)}, bf16[128,4096]{1,0:T(8,128)(2,1)}, u32[]{:S(2)}) copy-start(bf16[128,4096]{1,0:T(8,128)(2,1)} %copy-done.25) | copy-start | bytes 3145732
  311.8 14.7 %collective-permute-start.3 = (bf16[128,4096]{1,0:T(8,128)(2,1)}, bf16[128,4096]{1,0:T(8,128)(2,1)S(1)}, u32[]{:S(2)}, u32[]{:S(2)}) collective-permute-start(bf16[128,4096]{1,0:T(8,128)(2,1)} %bitcast.43), channel_id=1, source_target_pairs={{0,4},{4,8},{8,12},{1,5},{5,9},{9,13},{2,6},{6,10},{10,14},{3,7},{... | collective-permute-start | bytes 3145736 | tf_op jit(solution)/shard_map/ppermute | solution.py:44
  324.0 9.7 %slice-start = ((s8[6291456]{0:T(1024)(128)(4,1)}), s8[4194304]{0:T(1024)(128)(4,1)S(1)}, s32[]{:S(2)}) async-start(s8[6291456]{0:T(1024)(128)(4,1)} %bitcast.1138), calls=%async_computation.20 | async-start | bytes 8388608
  341.6 9.7 %copy-start.45 = (bf16[144,2,128]{2,0,1:T(8,128)(2,1)}, bf16[144,2,128]{2,0,1:T(8,128)(2,1)S(1)}, u32[]{:S(2)}) copy-start(bf16[144,2,128]{2,0,1:T(8,128)(2,1)S(1)} %fusion.343) | copy-start | bytes 221188
  343.3 7.9 copy-start.44
  355.9 14.4 %all-to-all-start.8 = ((bf16[4,32,4096]{2,1,0:T(8,128)(2,1)}), bf16[4,32,4096]{2,1,0:T(8,128)(2,1)S(1)}, u32[]{:S(2)}, u32[]{:S(2)}) async-start(bf16[4,32,4096]{2,1,0:T(8,128)(2,1)} %bitcast.1219), calls=%async_computation.8 | async-start | bytes 2097152 | tf_op jit(solution)/shard_map/all_to_all | solution.py:49
  359.4 55.7 %all-gather.10.cloned.1.call-start = ((), (), s32[]{:S(2)}) async-start(), calls=%async_computation.14 | async-start | bytes 1310720 | tf_op jit(solution)/shard_map/all_gather | solution.py:212
  371.7 12.6 %copy-start.19 = (bf16[1,128,4096]{2,1,0:T(8,128)(2,1)S(1)}, bf16[1,128,4096]{2,1,0:T(8,128)(2,1)}, u32[]{:S(2)}) copy-start(bf16[1,128,4096]{2,1,0:T(8,128)(2,1)} %get-tuple-element.27) | copy-start | bytes 3145732
  373.1 10.5 %collective-permute-start.4 = (bf16[32,4096]{1,0:T(8,128)(2,1)S(1)}, bf16[32,4096]{1,0:T(8,128)(2,1)S(1)}, u32[]{:S(2)}, u32[]{:S(2)}) collective-permute-start(bf16[32,4096]{1,0:T(8,128)(2,1)S(1)} %fusion.489), channel_id=1, source_target_pairs={{4,0},{8,4},{12,8},{5,1},{9,5},{13,9},{6,2},{10,6},{14,10},{7,3},{... | collective-permute-start | bytes 786440 | tf_op jit(solution)/shard_map/ppermute | solution.py:44
  447.9 17.7 %all-to-all-start.9 = ((bf16[4,32,4096]{2,1,0:T(8,128)(2,1)}), bf16[4,32,4096]{2,1,0:T(8,128)(2,1)}, u32[]{:S(2)}, u32[]{:S(2)}) async-start(bf16[4,32,4096]{2,1,0:T(8,128)(2,1)} %bitcast.1220), calls=%async_computation.9 | async-start | bytes 2097152 | tf_op jit(solution)/shard_map/all_to_all | solution.py:49
  452.3 49.8 %all-gather.12.cloned.1.call-start = ((), (), s32[]{:S(2)}) async-start(), calls=%async_computation.15 | async-start | bytes 1310720 | tf_op jit(solution)/shard_map/all_gather | solution.py:212
  469.8 3.4 collective-permute-start.5
  529.1 17.6 %all-to-all-start.10 = ((bf16[4,32,4096]{2,1,0:T(8,128)(2,1)}), bf16[4,32,4096]{2,1,0:T(8,128)(2,1)}, u32[]{:S(2)}, u32[]{:S(2)}) async-start(bf16[4,32,4096]{2,1,0:T(8,128)(2,1)} %bitcast.1218), calls=%async_computation.10 | async-start | bytes 2097152 | tf_op jit(solution)/shard_map/all_to_all | solution.py:49
  533.3 48.9 %all-gather.14.cloned.1.call-start = ((), (), s32[]{:S(2)}) async-start(), calls=%async_computation.16 | async-start | bytes 1310720 | tf_op jit(solution)/shard_map/all_gather | solution.py:212
  540.1 9.4 %copy-start.33 = (bf16[32,4096]{1,0:T(8,128)(2,1)S(1)}, bf16[32,4096]{1,0:T(8,128)(2,1)}, u32[]{:S(2)}) copy-start(bf16[32,4096]{1,0:T(8,128)(2,1)} %copy-done.32) | copy-start | bytes 786436
  550.8 3.9 collective-permute-start.6
  614.9 17.6 %all-to-all-start.11 = ((bf16[4,32,4096]{2,1,0:T(8,128)(2,1)}), bf16[4,32,4096]{2,1,0:T(8,128)(2,1)}, u32[]{:S(2)}, u32[]{:S(2)}) async-start(bf16[4,32,4096]{2,1,0:T(8,128)(2,1)} %bitcast.1217), calls=%async_computation.11 | async-start | bytes 2097152 | tf_op jit(solution)/shard_map/all_to_all | solution.py:49
  619.2 50.8 %all-gather.16.cloned.1.call-start = ((), (), s32[]{:S(2)}) async-start(), calls=%async_computation.17 | async-start | bytes 1310720 | tf_op jit(solution)/shard_map/all_gather | solution.py:212
  637.2 4.6 collective-permute-start.7
  653.0 22.5 %copy-start.43 = (bf16[128,768]{0,1:T(8,128)(2,1)S(1)}, bf16[128,768]{0,1:T(8,128)(2,1)}, u32[]{:S(2)}) copy-start(bf16[128,768]{0,1:T(8,128)(2,1)} %copy.304) | copy-start | bytes 589828
  653.0 22.5 %copy-start.115 = (f32[2,3,128]{2,1,0:T(4,128)S(1)}, f32[2,3,128]{2,1,0:T(4,128)}, u32[]{:S(2)}) copy-start(f32[2,3,128]{2,1,0:T(4,128)} %get-tuple-element.37) | copy-start | bytes 9220
  676.9 9.0 %copy-start.39 = (f32[1,64,256]{2,1,0:T(8,128)S(1)}, f32[1,64,256]{2,1,0:T(8,128)}, u32[]{:S(2)}) copy-start(f32[1,64,256]{2,1,0:T(8,128)} %convolution_bitcast_fusion.23) | copy-start | bytes 196612
  676.9 9.0 %copy-start.40 = (f32[1,64,256]{2,1,0:T(8,128)S(1)}, f32[1,64,256]{2,1,0:T(8,128)}, u32[]{:S(2)}) copy-start(f32[1,64,256]{2,1,0:T(8,128)} %convolution_bitcast_fusion.24) | copy-start | bytes 196612
  677.4 15.4 %copy-start.30 = (bf16[2,16,4096]{2,1,0:T(8,128)(2,1)S(1)}, bf16[2,16,4096]{2,1,0:T(8,128)(2,1)}, u32[]{:S(2)}) copy-start(bf16[2,16,4096]{2,1,0:T(8,128)(2,1)} %fusion.579) | copy-start | bytes 786436
  682.2 9.2 %all-to-all-start.12 = ((f32[4,1,4096]{2,1,0:T(1,128)}), f32[4,1,4096]{2,1,0:T(1,128)S(1)}, u32[]{:S(2)}, u32[]{:S(2)}) async-start(f32[4,1,4096]{2,1,0:T(1,128)} %reshape.1704), calls=%async_computation.12 | async-start | bytes 131072 | tf_op jit(solution)/shard_map/all_to_all | solution.py:34
  685.8 88.8 %all-reduce.2.cloned.1.call-start = ((), (), s32[]{:S(2)}) async-start(), calls=%async_computation.18 | async-start | bytes 131072 | tf_op jit(solution)/shard_map/psum | solution.py:262
  686.6 195.1 %all-gather.18.cloned.1.call-start = ((), (), s32[]{:S(2)}) async-start(), calls=%async_computation.19 | async-start | bytes 9437184 | tf_op jit(solution)/shard_map/all_gather | solution.py:261
  (99 other events, 377.7 us)
Sparse Core Ops, SparseCore 0:
  11.1 26.9 all-gather.7
  385.2 29.8 all-gather.9
  474.8 27.2 all-gather.11
  555.6 26.6 all-gather.13
  643.7 26.3 all-gather.15
  688.8 85.7 all-reduce.1
  777.5 104.0 all-gather.17
